TPU v7x, 32 devices: a whole 2x2x4 slice. The times are simulated.
32 devices in a mesh: groups: 2 (over y), region: 4 (over z), head: 4 (over x, core).
Axes of the slice: x: 2, y: 2, z: 4, core: 2. Of those that a mesh axis runs over, the one named last changes fastest.
Arguments:
- video_queries: bfloat16 [2, 4, 256, 3072], P('groups', 'region', None, 'head'), parts along dimension 0, may hold values from -6 to 6
- video_keys: bfloat16 [2, 4, 256, 3072], P('groups', 'region', None, 'head'), parts along dimension 0, may hold values from -6 to 6
- video_values: bfloat16 [2, 4, 256, 3072], P('groups', 'region', None, 'head'), parts along dimension 0, may hold values from -12 to 12
- head_window: int32 [24, 2], P('head'), may hold values from 0 to 1
- prompt_keys: bfloat16 [512, 3072], P(('groups', 'region'), 'head'), parts along dimension 0, may hold values from -10 to 10
- prompt_values: bfloat16 [512, 3072], P(('groups', 'region'), 'head'), parts along dimension 0, may hold values from -10 to 10
- text_len: int32 [2], P('groups'), parts along dimension 0, may hold values from 64 to 256
Outputs:
- attended: bfloat16 [2, 4, 256, 3072], P('groups', 'region', None, 'head'), parts along dimension 0
There are 2 independent parts, one for each index of `groups`. A program takes and returns all parts, laid end to end along the dimension named above; an argument that names none is the same for every part. Nothing has to cross between parts.
Inputs may be any that keep to these rules, and one draw needn't show every extreme that they name: `head_window`: entry (h, 0) is head h's reach in tiles along grid rows, (h, 1) along grid columns; the window spans 2 r + 1 tiles along each. The first text_len[0] of the 256 prompt tokens are live.
All inputs are finite; a program needn't handle non-finite values.
Results may differ from a plain program's by a relative error of at most 0.0035.
Values may be sent and summed in bfloat16 or wider, within the bound.
A program may use at most 128 MiB of HBM per device.

v0:
```python
import math

import jax
import jax.numpy as jnp
from jax import lax
from jax.sharding import PartitionSpec as P


def absorb(softmax_state, query_heads, block_keys, block_values, allowed):
    running_max, running_sum, weighted = softmax_state
    score_scale = 1.0 / math.sqrt(query_heads.shape[-1])
    scores = (
        jnp.einsum("sqhd,skhd->shqk", query_heads, block_keys, preferred_element_type=jnp.float32)
        * score_scale
    )
    scores = jnp.where(allowed, scores, -jnp.inf)
    new_max = jnp.maximum(running_max, jnp.max(scores, axis=-1, keepdims=True))
    weights = jnp.exp(scores - new_max)
    rescale = jnp.exp(running_max - new_max)
    running_sum = running_sum * rescale + jnp.sum(weights, axis=-1, keepdims=True)
    contribution = jnp.einsum(
        "shqk,skhd->sqhd",
        weights.astype(jnp.bfloat16),
        block_values,
        preferred_element_type=jnp.float32,
    )
    weighted = weighted * jnp.transpose(rescale, (0, 2, 1, 3)) + contribution
    return (new_max, running_sum, weighted)


def shards(
    video_queries, video_keys, video_values, head_window, prompt_keys, prompt_values, text_len
):
    slab_count = video_queries.shape[0]
    tile_tok = video_queries.shape[2]
    features = video_queries.shape[3]
    head_count = head_window.shape[0]
    head_dim = features // head_count
    region_count = lax.axis_size("region")
    grid_cols = min(8, region_count // 2)
    position = lax.axis_index("region")
    my_row = position // grid_cols
    my_col = position % grid_cols
    reach_rows = head_window[:, 0]
    reach_cols = head_window[:, 1]
    query_heads = video_queries.reshape(slab_count, tile_tok, head_count, head_dim)
    paired = jnp.stack([video_keys, video_values])
    stat_shape = (slab_count, head_count, tile_tok, 1)
    softmax_state = (
        jnp.full(stat_shape, -1e30, jnp.float32),
        jnp.zeros(stat_shape, jnp.float32),
        jnp.zeros((slab_count, tile_tok, head_count, head_dim), jnp.float32),
    )
    shard_piece = lax.all_gather(paired, "region", axis=2, tiled=True)
    piece_count = shard_piece.shape[2]

    def one_tile(tile_slot, state_in):
        row_step = tile_slot // grid_cols - my_row
        col_step = tile_slot % grid_cols - my_col
        within = (jnp.abs(row_step) <= reach_rows) & (jnp.abs(col_step) <= reach_cols)
        tile_pair = lax.dynamic_slice_in_dim(shard_piece, tile_slot, 1, 2)
        block_keys = tile_pair[0].reshape(slab_count, tile_tok, head_count, head_dim)
        block_values = tile_pair[1].reshape(slab_count, tile_tok, head_count, head_dim)
        allowed = within.reshape(1, head_count, 1, 1)

        def take_tile(state_keep):
            return absorb(state_keep, query_heads, block_keys, block_values, allowed)

        def keep_state(state_keep):
            return state_keep

        return lax.cond(jnp.any(within), take_tile, keep_state, state_in)

    softmax_state = lax.fori_loop(0, piece_count, one_tile, softmax_state)
    live_text = text_len[0]
    prompt_piece = (
        lax.all_gather(prompt_keys, "region", axis=0, tiled=True),
        lax.all_gather(prompt_values, "region", axis=0, tiled=True),
    )
    piece_count = prompt_piece[0].shape[0]
    block_keys = prompt_piece[0].reshape(1, piece_count, head_count, head_dim)
    block_values = prompt_piece[1].reshape(1, piece_count, head_count, head_dim)
    allowed = (jnp.arange(piece_count, dtype=jnp.int32) < live_text).reshape(1, 1, 1, piece_count)
    softmax_state = absorb(softmax_state, query_heads, block_keys, block_values, allowed)
    running_max, running_sum, weighted = softmax_state
    result = weighted / jnp.transpose(running_sum, (0, 2, 1, 3))
    return result.reshape(slab_count, 1, tile_tok, features).astype(jnp.bfloat16)


def solution(mesh):
    in_specs = (
        P("groups", "region", None, "head"),
        P("groups", "region", None, "head"),
        P("groups", "region", None, "head"),
        P("head", None),
        P(("groups", "region"), "head"),
        P(("groups", "region"), "head"),
        P("groups"),
    )
    out_specs = P("groups", "region", None, "head")
    return jax.shard_map(shards, mesh=mesh, in_specs=in_specs, out_specs=out_specs, check_vma=False)
```

profile of v0, /device:TPU:0, one launch (start us, length us, event | category | flops | bytes accessed | tf_op | source)
XLA Modules:
  0.0 107.9 jit_solution(6140674785394335826)
XLA Ops:
  6.5 1.2 %copy.30 = bf16[1,1,256,768]{2,3,1,0:T(8,128)(2,1)S(1)} copy(bf16[1,1,256,768]{3,2,1,0:T(8,128)(2,1)} %param.12) | data formatting | bytes 786432 | tf_op args[1]
  7.7 1.2 %copy.31 = bf16[1,1,256,768]{2,3,1,0:T(8,128)(2,1)S(1)} copy(bf16[1,1,256,768]{3,2,1,0:T(8,128)(2,1)} %param.13) | data formatting | bytes 786432 | tf_op args[2]
  8.9 0.9 pad_maximum_fusion
  10.8 18.0 %all_gather.10 = bf16[256,768]{1,0:T(8,128)(2,1)S(1)} all-gather(bf16[64,768]{1,0:T(8,128)(2,1)S(1)} %copy-done.1), channel_id=1, replica_groups=mesh['groups'=2,'region'=4,'head'=4] {'region'}, dimensions={0}, use_global_device_ids=true | all-gather | bytes 491520 | tf_op jit(solution)/shard_map/all_gather | solution.py:77
  29.6 20.2 %all_gather.11 = bf16[256,768]{1,0:T(8,128)(2,1)S(1)} all-gather(bf16[64,768]{1,0:T(8,128)(2,1)S(1)} %copy-done.2), channel_id=1, replica_groups=mesh['groups'=2,'region'=4,'head'=4] {'region'}, dimensions={0}, use_global_device_ids=true | all-gather | bytes 491520 | tf_op jit(solution)/shard_map/all_gather | solution.py:78
  50.5 33.3 %all-gather.2.cloned.1.call-done = bf16[2,1,4,256,768]{3,4,2,1,0:T(8,128)(2,1)} async-done(((bf16[2,1,1,256,768]{3,4,2,1,0:T(8,128)(2,1)}), bf16[2,1,4,256,768]{3,4,2,1,0:T(8,128)(2,1)}) %all-gather.2.cloned.1.call-update) | async-done | bytes 3145744 | tf_op jit(solution)/shard_map/all_gather | solution.py:54
  83.9 15.6 %while.19 = (s32[]{:T(128)}, f32[1,6,256,1]{2,1,3,0:T(8,128)S(1)}, f32[1,6,256,1]{2,1,3,0:T(8,128)S(1)}, f32[1,256,6,128]{1,3,2,0:T(8,128)S(1)}, s32[]{:T(128)},...) while((s32[]{:T(128)}, f32[1,6,256,1]{2,1,3,0:T(8,128)S(1)}, ...), condition=%wide.region_6.7_spmd, body=%wide.region_0.6_spmd.sunk | while | flops 204476992 | bytes 9142846 | solution.py:74
  83.9 0.7 and_reduce_fusion.2
  85.3 2.5 %conditional.2 = ((f32[1,6,256,1]{2,1,3,0:T(8,128)S(1)}, f32[1,6,256,1]{2,1,3,0:T(8,128)S(1)}, f32[1,256,6,128]{1,3,2,0:T(8,128)S(1)})) conditional(s32[]{:T(128)} %convert_element_type.43, (f32[1,6,256,1]{2,1,3,0:T(8,128)S(1)}, f32[1,6,256,1]{2,1,3,0:T(8,128)S(1)}, f32[1,256,6,128]{1,3,2,0:T(8,128)S(1)}) %tuple.58, (s32[]{:T(128)}, s32[6]{0:T(128)S(1)}, ...), branch_computations={%region_2.2_spmd, %region_3.5_spmd} | conditional | flops 204476944 | bytes 9142392 | solution.py:72
  85.3 1.2 %constant_dynamic-slice_fusion.1 = (bf16[1,1,1,256,768]{3,4,2,1,0:T(8,128)(2,1)S(1)}, bf16[1,1,1,256,768]{3,4,2,1,0:T(8,128)(2,1)S(1)}) fusion(bf16[2,1,4,256,768]{3,4,2,1,0:T(8,128)(2,1)} %get-tuple-element.353, s32[]{:T(128)S(6)} %add.74, s32[]{:T(128)} %get-tuple-element.354), kind=kLoop, calls=%fused_computation.16 | loop fusion | bytes 1572872 | tf_op jit(solution)/shard_map/while/body/eval_jaxpr/slice | solution.py:63
  87.2 0.6 fusion.3
  87.8 0.7 and_reduce_fusion.2
  89.2 2.5 %conditional.2 = ((f32[1,6,256,1]{2,1,3,0:T(8,128)S(1)}, f32[1,6,256,1]{2,1,3,0:T(8,128)S(1)}, f32[1,256,6,128]{1,3,2,0:T(8,128)S(1)})) conditional(s32[]{:T(128)} %convert_element_type.43, (f32[1,6,256,1]{2,1,3,0:T(8,128)S(1)}, f32[1,6,256,1]{2,1,3,0:T(8,128)S(1)}, f32[1,256,6,128]{1,3,2,0:T(8,128)S(1)}) %tuple.58, (s32[]{:T(128)}, s32[6]{0:T(128)S(1)}, ...), branch_computations={%region_2.2_spmd, %region_3.5_spmd} | conditional | flops 204476944 | bytes 9142392 | solution.py:72
  89.2 1.2 %constant_dynamic-slice_fusion.1 = (bf16[1,1,1,256,768]{3,4,2,1,0:T(8,128)(2,1)S(1)}, bf16[1,1,1,256,768]{3,4,2,1,0:T(8,128)(2,1)S(1)}) fusion(bf16[2,1,4,256,768]{3,4,2,1,0:T(8,128)(2,1)} %get-tuple-element.353, s32[]{:T(128)S(6)} %add.74, s32[]{:T(128)} %get-tuple-element.354), kind=kLoop, calls=%fused_computation.16 | loop fusion | bytes 1572872 | tf_op jit(solution)/shard_map/while/body/eval_jaxpr/slice | solution.py:63
  91.1 0.6 fusion.3
  91.7 0.7 and_reduce_fusion.2
  93.1 2.5 %conditional.2 = ((f32[1,6,256,1]{2,1,3,0:T(8,128)S(1)}, f32[1,6,256,1]{2,1,3,0:T(8,128)S(1)}, f32[1,256,6,128]{1,3,2,0:T(8,128)S(1)})) conditional(s32[]{:T(128)} %convert_element_type.43, (f32[1,6,256,1]{2,1,3,0:T(8,128)S(1)}, f32[1,6,256,1]{2,1,3,0:T(8,128)S(1)}, f32[1,256,6,128]{1,3,2,0:T(8,128)S(1)}) %tuple.58, (s32[]{:T(128)}, s32[6]{0:T(128)S(1)}, ...), branch_computations={%region_2.2_spmd, %region_3.5_spmd} | conditional | flops 204476944 | bytes 9142392 | solution.py:72
  93.1 1.2 %constant_dynamic-slice_fusion.1 = (bf16[1,1,1,256,768]{3,4,2,1,0:T(8,128)(2,1)S(1)}, bf16[1,1,1,256,768]{3,4,2,1,0:T(8,128)(2,1)S(1)}) fusion(bf16[2,1,4,256,768]{3,4,2,1,0:T(8,128)(2,1)} %get-tuple-element.353, s32[]{:T(128)S(6)} %add.74, s32[]{:T(128)} %get-tuple-element.354), kind=kLoop, calls=%fused_computation.16 | loop fusion | bytes 1572872 | tf_op jit(solution)/shard_map/while/body/eval_jaxpr/slice | solution.py:63
  95.0 0.6 fusion.3
  95.6 0.7 and_reduce_fusion.2
  97.0 2.5 %conditional.2 = ((f32[1,6,256,1]{2,1,3,0:T(8,128)S(1)}, f32[1,6,256,1]{2,1,3,0:T(8,128)S(1)}, f32[1,256,6,128]{1,3,2,0:T(8,128)S(1)})) conditional(s32[]{:T(128)} %convert_element_type.43, (f32[1,6,256,1]{2,1,3,0:T(8,128)S(1)}, f32[1,6,256,1]{2,1,3,0:T(8,128)S(1)}, f32[1,256,6,128]{1,3,2,0:T(8,128)S(1)}) %tuple.58, (s32[]{:T(128)}, s32[6]{0:T(128)S(1)}, ...), branch_computations={%region_2.2_spmd, %region_3.5_spmd} | conditional | flops 204476944 | bytes 9142392 | solution.py:72
  97.0 1.2 %constant_dynamic-slice_fusion.1 = (bf16[1,1,1,256,768]{3,4,2,1,0:T(8,128)(2,1)S(1)}, bf16[1,1,1,256,768]{3,4,2,1,0:T(8,128)(2,1)S(1)}) fusion(bf16[2,1,4,256,768]{3,4,2,1,0:T(8,128)(2,1)} %get-tuple-element.353, s32[]{:T(128)S(6)} %add.74, s32[]{:T(128)} %get-tuple-element.354), kind=kLoop, calls=%fused_computation.16 | loop fusion | bytes 1572872 | tf_op jit(solution)/shard_map/while/body/eval_jaxpr/slice | solution.py:63
  98.9 0.6 fusion.3
  100.2 0.9 copy.40
  (48 shorter events, 5.1 us)
Async XLA Ops:
  6.5 77.2 %all-gather.2.cloned.1.call-start = ((), (), s32[]{:S(2)}) async-start(), calls=%async_computation | async-start | bytes 3932160 | tf_op jit(solution)/shard_map/all_gather | solution.py:54
  7.7 2.2 %copy-start = (bf16[1,1,256,768]{3,2,1,0:T(8,128)(2,1)S(1)}, bf16[1,1,256,768]{3,2,1,0:T(8,128)(2,1)}, u32[]{:S(2)}) copy-start(bf16[1,1,256,768]{3,2,1,0:T(8,128)(2,1)} %param.11) | copy-start | bytes 1179652
  9.9 0.9 copy-start.1
  9.9 19.7 %copy-start.2 = (bf16[64,768]{1,0:T(8,128)(2,1)S(1)}, bf16[64,768]{1,0:T(8,128)(2,1)}, u32[]{:S(2)}) copy-start(bf16[64,768]{1,0:T(8,128)(2,1)} %param.16) | copy-start | bytes 294916
  10.1 39.9 %copy-start.3 = (s32[6,2]{0,1:T(2,128)S(1)}, s32[6,2]{0,1:T(2,128)}, u32[]{:S(2)}) copy-start(s32[6,2]{0,1:T(2,128)} %param.14) | copy-start | bytes 148
Sparse Core Ops, SparseCore 0:
  10.0 73.7 all-gather.1
where the time goes:
time: 108 us
  blocking collectives  38.2 us (35%)
  waiting for transfers between devices  33.3 us (31%)
  between operations  14.2 us (13%)
  local copies, waits for them, and re-layouts  9.24 us (9%)
  other arithmetic  4.98 us (5%)
  matrix products  4.77 us (4%)
  loops' own time  3.17 us (3%)
    all_gather x1, waiting for transfers between devices, shards(): shard_piece = lax.all_gather(paired, 'region', axis=2, tiled=True)  33.3 us
    all_gather x1, blocking collectives, shards(): lax.all_gather(prompt_values, 'region', axis=0, tiled=True)  20.2 us
    all_gather x1, blocking collectives, shards(): lax.all_gather(prompt_keys, 'region', axis=0, tiled=True)  18 us
    slice x4, local copies, waits for them, and re-layouts, one_tile(): tile_pair[1].reshape(slab_count, tile_tok, head_count, head_dim)  4.7 us
    unnamed x11, local copies, waits for them, and re-layouts  2.98 us
    another operation x1, loops' own time, shards(): softmax_state = lax.fori_loop(0, piece_count, one_tile, softmax_state)  2.89 us
    reduce_or x4, other arithmetic, one_tile(): return lax.cond(jnp.any(within), take_tile, keep_state, state_in)  2.79 us
    dot_general x5, matrix products, absorb(): jnp.einsum('shqk,skhd->sqhd', weights.astype(jnp.bfloat16), block_values,...  2.63 us
  transfers between devices with their start and end apart: 1, of which 1 were waited for; matrix products, arithmetic and copies ran while one was open for 1% of the time, Pallas kernels for 0%

commit v1 on v0

--- a/solution.py
+++ b/solution.py
@@ -1,9 +1,16 @@
+import functools
 import math
 
 import jax
 import jax.numpy as jnp
 from jax import lax
+from jax.experimental import pallas as pl
+from jax.experimental.pallas import tpu as pltpu
 from jax.sharding import PartitionSpec as P
+
+MESH = pl.DeviceIdType.MESH
+MASKED = -1e30
+VMEM_BUDGET = 24 * 2**20
 
 
 def absorb(softmax_state, query_heads, block_keys, block_values, allowed):
@@ -28,7 +35,7 @@
     return (new_max, running_sum, weighted)
 
 
-def shards(
+def gathered(
     video_queries, video_keys, video_values, head_window, prompt_keys, prompt_values, text_len
 ):
     slab_count = video_queries.shape[0]
@@ -87,6 +94,327 @@
     return result.reshape(slab_count, 1, tile_tok, features).astype(jnp.bfloat16)
 
 
+def attend(queries, blocks, score_scale):
+    scores = [
+        lax.dot_general(
+            queries, keys, (((1,), (1,)), ((), ())), preferred_element_type=jnp.float32
+        )
+        + bias
+        for keys, _, bias in blocks
+    ]
+    row_max = jnp.max(functools.reduce(jnp.maximum, scores), axis=-1, keepdims=True)
+    weights = [jnp.exp2((block - row_max) * (score_scale / math.log(2.0))) for block in scores]
+    row_sum = jnp.sum(functools.reduce(jnp.add, weights), axis=-1, keepdims=True)
+    weighted = functools.reduce(
+        jnp.add,
+        [
+            jnp.dot(weight.astype(jnp.bfloat16), values, preferred_element_type=jnp.float32)
+            for weight, (_, values, _) in zip(weights, blocks)
+        ],
+    )
+    return (weighted * (1.0 / row_sum)).astype(jnp.bfloat16)
+
+
+def exchange_kernel(
+    dims,
+    window_ref, text_len_ref, q_ref, k_ref, v_ref, tk_ref, tv_ref, out_ref,
+    q_own, k_own, v_own, tk_own, tv_own, o_out, o_land,
+    q_rest, k_rest, v_rest, tk_rest, tv_rest,
+    own_send, own_recv, rest_send, rest_recv, relay_send, o_send, o_recv, local_sem,
+):
+    n, heads, head_dim, grid_cols = dims
+    me = lax.axis_index("region")
+    per_device = heads // n
+    rest = heads - per_device * n
+    width = per_device * head_dim
+    rest_cols = pl.ds(n * width, rest * head_dim)
+    half = n // 2
+    score_scale = 1.0 / math.sqrt(head_dim)
+
+    barrier = pltpu.get_barrier_semaphore()
+    for step in range(1, n):
+        pl.semaphore_signal(
+            barrier, inc=1, device_id={"region": lax.rem(me + step, n)}, device_id_type=MESH
+        )
+
+    def columns(owner):
+        return pl.ds(pl.multiple_of(owner * width, head_dim), width)
+
+    own_pairs = ((k_ref, k_own), (q_ref, q_own), (tk_ref, tk_own), (v_ref, v_own), (tv_ref, tv_own))
+    rest_pairs = ((k_ref, k_rest), (v_ref, v_rest), (tk_ref, tk_rest), (tv_ref, tv_rest))
+
+    local = [
+        pltpu.make_async_copy(src.at[:, columns(me)], dst.at[me], local_sem.at[i])
+        for i, (src, dst) in enumerate(own_pairs)
+    ]
+    if rest:
+        local += [
+            pltpu.make_async_copy(src.at[:, rest_cols], dst.at[me], local_sem.at[5 + i])
+            for i, (src, dst) in enumerate(rest_pairs)
+        ]
+        local.append(pltpu.make_async_copy(q_ref.at[:, rest_cols], q_rest, local_sem.at[9]))
+    for copy in local:
+        copy.start()
+
+    def own_copy(target, source, slot, i):
+        src, dst = own_pairs[i]
+        return pltpu.make_async_remote_copy(
+            src_ref=src.at[:, columns(target)],
+            dst_ref=dst.at[source],
+            send_sem=own_send.at[slot, i],
+            recv_sem=own_recv.at[source, i],
+            device_id={"region": target},
+            device_id_type=MESH,
+        )
+
+    def rest_copy(target, source, i):
+        src, dst = rest_pairs[i]
+        return pltpu.make_async_remote_copy(
+            src_ref=src.at[:, rest_cols],
+            dst_ref=dst.at[source],
+            send_sem=rest_send.at[target, i],
+            recv_sem=rest_recv.at[source, i],
+            device_id={"region": target},
+            device_id_type=MESH,
+        )
+
+    def relay_copy(target, source, i):
+        dst = rest_pairs[i][1]
+        return pltpu.make_async_remote_copy(
+            src_ref=dst.at[source],
+            dst_ref=dst.at[source],
+            send_sem=relay_send.at[source, target, i],
+            recv_sem=rest_recv.at[source, i],
+            device_id={"region": target},
+            device_id_type=MESH,
+        )
+
+    def o_copy(target, source, slot):
+        return pltpu.make_async_remote_copy(
+            src_ref=o_out.at[target],
+            dst_ref=o_land.at[source],
+            send_sem=o_send.at[slot],
+            recv_sem=o_recv.at[source],
+            device_id={"region": target},
+            device_id_type=MESH,
+        )
+
+    def same_half(target):
+        return (me != target) & ((me < half) == (target < half))
+
+    def relay_far(target):
+        return (me < half) != (target < half)
+
+    relays = (half - 1, half)
+    order = sorted(range(1, n), key=lambda step: abs(step - half))
+
+    pl.semaphore_wait(barrier, n - 1)
+    if rest:
+        for target in relays:
+
+            @pl.when(relay_far(target))
+            def _(target=target):
+                for i in range(4):
+                    rest_copy(target, me, i).start()
+
+    for step in order:
+        for i in range(5):
+            own_copy(lax.rem(me + step, n), me, step, i).start()
+    if rest:
+        for target in range(n):
+
+            @pl.when(same_half(target))
+            def _(target=target):
+                for i in range(4):
+                    rest_copy(target, me, i).start()
+
+        for relay in relays:
+            near = range(half) if relay < half else range(half, n)
+            far = range(half, n) if relay < half else range(half)
+
+            @pl.when(me == relay)
+            def _(relay=relay, near=near, far=far):
+                for source in far:
+                    for i in range(4):
+                        rest_copy(relay, source, i).wait_recv()
+                        for target in near:
+                            if target != relay:
+                                relay_copy(target, source, i).start()
+
+    for copy in local:
+        copy.wait()
+    text_bias = jnp.where(
+        lax.broadcasted_iota(jnp.int32, (1, n * tk_ref.shape[0]), 1) < text_len_ref[0], 0.0, MASKED
+    )
+
+    def tile_bias(head, tile_q, tile_k):
+        rows = jnp.abs(tile_q // grid_cols - tile_k // grid_cols)
+        cols = jnp.abs(tile_q % grid_cols - tile_k % grid_cols)
+        within = (rows <= window_ref[head, 0]) & (cols <= window_ref[head, 1])
+        return jnp.where(within, 0.0, MASKED)
+
+    def blocks_of(keys, values, text_keys, text_values, local_head, head, tile_q):
+        lanes = pl.ds(local_head * head_dim, head_dim)
+        blocks = [
+            (keys[t, :, lanes], values[t, :, lanes], tile_bias(head, tile_q, t)) for t in range(n)
+        ]
+        blocks.append(
+            (
+                text_keys[:, :, lanes].reshape(-1, head_dim),
+                text_values[:, :, lanes].reshape(-1, head_dim),
+                text_bias,
+            )
+        )
+        return blocks
+
+    for step in order:
+        for i in range(5):
+            own_copy(me, lax.rem(me + step, n), step, i).wait_recv()
+    for step in order + [0]:
+        tile = lax.rem(me + step, n)
+        for local_head in range(per_device):
+            lanes = pl.ds(local_head * head_dim, head_dim)
+            result = attend(
+                q_own[tile, :, lanes],
+                blocks_of(
+                    k_own, v_own, tk_own, tv_own, local_head, me * per_device + local_head, tile
+                ),
+                score_scale,
+            )
+            if step:
+                o_out[tile, :, lanes] = result
+            else:
+                o_land[me, :, lanes] = result
+        if step:
+            o_copy(tile, me, step).start()
+
+    if rest:
+        for source in range(n):
+            received = (me != source) & ((me < half) == (source < half))
+            if True:
+
+                @pl.when(received)
+                def _(source=source):
+                    for i in range(4):
+                        rest_copy(me, source, i).wait_recv()
+
+                @pl.when(relay_far(source) & (me != half - 1) & (me != half))
+                def _(source=source):
+                    for i in range(4):
+                        rest_copy(me, source, i).wait_recv()
+
+        for local_head in range(rest):
+            lanes = pl.ds(local_head * head_dim, head_dim)
+            out_ref[:, pl.ds(n * width + local_head * head_dim, head_dim)] = attend(
+                q_rest[:, lanes],
+                blocks_of(
+                    k_rest, v_rest, tk_rest, tv_rest, local_head, n * per_device + local_head, me
+                ),
+                score_scale,
+            )
+
+    for step in order:
+        o_copy(me, lax.rem(me + step, n), step).wait_recv()
+    for owner in range(n):
+        out_ref[:, pl.ds(owner * width, width)] = o_land[owner]
+
+    for step in order:
+        for i in range(5):
+            own_copy(lax.rem(me + step, n), me, step, i).wait_send()
+        o_copy(lax.rem(me + step, n), me, step).wait_send()
+    if rest:
+        for target in range(n):
+
+            @pl.when(same_half(target) | (relay_far(target) & (target in relays)))
+            def _(target=target):
+                for i in range(4):
+                    rest_copy(target, me, i).wait_send()
+
+        for relay in relays:
+            near = range(half) if relay < half else range(half, n)
+            far = range(half, n) if relay < half else range(half)
+
+            @pl.when(me == relay)
+            def _(relay=relay, near=near, far=far):
+                for source in far:
+                    for i in range(4):
+                        for target in near:
+                            if target != relay:
+                                relay_copy(target, source, i).wait_send()
+
+
+def exchange(
+    video_queries, video_keys, video_values, head_window, prompt_keys, prompt_values, text_len
+):
+    n = lax.axis_size("region")
+    tile_tok, features = video_queries.shape[2:]
+    text_tok = prompt_keys.shape[0]
+    heads = head_window.shape[0]
+    head_dim = features // heads
+    per_device = heads // n
+    width = per_device * head_dim
+    rest_width = max(features - n * width, head_dim)
+    grid_cols = min(8, n // 2)
+    kind = video_queries.dtype
+    any_spec = pl.BlockSpec(memory_space=pl.ANY)
+    smem_spec = pl.BlockSpec(memory_space=pltpu.SMEM)
+    tile_own = pltpu.VMEM((n, tile_tok, width), kind)
+    text_own = pltpu.VMEM((n, text_tok, width), kind)
+    tile_rest = pltpu.VMEM((n, tile_tok, rest_width), kind)
+    text_rest = pltpu.VMEM((n, text_tok, rest_width), kind)
+    dma = pltpu.SemaphoreType.DMA
+    keys_total = n * (tile_tok + text_tok)
+    result = pl.pallas_call(
+        functools.partial(exchange_kernel, (n, heads, head_dim, grid_cols)),
+        out_shape=jax.ShapeDtypeStruct((tile_tok, features), kind),
+        in_specs=[smem_spec, smem_spec] + [any_spec] * 5,
+        out_specs=pl.BlockSpec(memory_space=pltpu.VMEM),
+        scratch_shapes=[
+            tile_own, tile_own, tile_own, text_own, text_own, tile_own, tile_own,
+            pltpu.VMEM((tile_tok, rest_width), kind),
+            tile_rest, tile_rest, text_rest, text_rest,
+            dma((n, 5)), dma((n, 5)), dma((n, 4)), dma((n, 4)), dma((n, n, 4)),
+            dma((n,)), dma((n,)), dma((10,)),
+        ],
+        compiler_params=pltpu.CompilerParams(collective_id=0, has_side_effects=True),
+        cost_estimate=pl.CostEstimate(
+            flops=4 * tile_tok * features * keys_total,
+            bytes_accessed=8 * tile_tok * features * n,
+            transcendentals=tile_tok * heads * keys_total,
+        ),
+        name="exchange_attend",
+    )(
+        head_window,
+        text_len,
+        video_queries.reshape(tile_tok, features),
+        video_keys.reshape(tile_tok, features),
+        video_values.reshape(tile_tok, features),
+        prompt_keys,
+        prompt_values,
+    )
+    return result.reshape(video_queries.shape)
+
+
+def fits(video_queries, head_window):
+    n = lax.axis_size("region")
+    heads = head_window.shape[0]
+    slabs, tiles, tile_tok, features = video_queries.shape
+    landed = 12 * n * tile_tok * features
+    return (
+        slabs == 1 and tiles == 1 and n % 2 == 0 and heads >= n
+        and features // heads == 128 and landed < VMEM_BUDGET
+    )
+
+
+def shards(
+    video_queries, video_keys, video_values, head_window, prompt_keys, prompt_values, text_len
+):
+    route = exchange if fits(video_queries, head_window) else gathered
+    return route(
+        video_queries, video_keys, video_values, head_window, prompt_keys, prompt_values, text_len
+    )
+
+
 def solution(mesh):
     in_specs = (
         P("groups", "region", None, "head"),

time: 108 us -> 57.4 us (0.53)
  Pallas kernels: 0 us -> 53.5 us
  blocking collectives: 38.2 us -> 0 us
  waiting for transfers between devices: 33.3 us -> 0 us
  between operations: 14.2 us -> 0.67 us
  local copies, waits for them, and re-layouts: 9.24 us -> 3.12 us
  other arithmetic: 4.98 us -> 0 us
  matrix products: 4.77 us -> 0 us
  loops' own time: 3.17 us -> 0 us
    pallas_call x0 -> x1, Pallas kernels: none -> 53.5 us  [exchange(): pl.pallas_call(functools.partial(exchange_kernel, (n, heads, head_dim, gr...]
    all_gather x2 -> x0, blocking collectives: 38.2 us -> none  [the longest x1 20.2 us: shards(): lax.all_gather(prompt_values, 'region', axis=0, tiled=True)]
    all_gather x1 -> x0, waiting for transfers between devices: 33.3 us -> none  [shards(): shard_piece = lax.all_gather(paired, 'region', axis=2, tiled=True)]
    dot_general x10 -> x0, matrix products: 4.77 us -> none  [the longest x5 2.63 us: absorb(): jnp.einsum('shqk,skhd->sqhd', weights.astype(jnp.bfloat16), block_values,...]
    slice x4 -> x0, local copies, waits for them, and re-layouts: 4.7 us -> none  [one_tile(): tile_pair[1].reshape(slab_count, tile_tok, head_count, head_dim)]
    another operation x5 -> x0, loops' own time: 3.17 us -> none  [the longest x1 2.89 us: shards(): softmax_state = lax.fori_loop(0, piece_count, one_tile, softmax_state)]
    reduce_or x4 -> x0, other arithmetic: 2.79 us -> none  [one_tile(): return lax.cond(jnp.any(within), take_tile, keep_state, state_in)]
    reduce_sum x5 -> x0, other arithmetic: 1.11 us -> none  [absorb(): jnp.sum(weights, axis=-1, keepdims=True)]
  transfers between devices with their start and end apart: 1 -> 0, of which waited for: 1 -> 0; matrix products, arithmetic and copies ran while one was open for 1% -> 0% of each run, Pallas kernels for 0% -> 0%
where the time goes in v1:
time: 57.4 us; the launch traced here: 57.2 us
  Pallas kernels  53.5 us (93%)
  local copies, waits for them, and re-layouts  3.12 us (5%)
  between operations  0.67 us (1%)
    pallas_call x1, Pallas kernels, exchange(): pl.pallas_call(functools.partial(exchange_kernel, (n, heads, head_dim, gr...  53.5 us
    unnamed x4, local copies, waits for them, and re-layouts  3.12 us

profile of v1, /device:TPU:0, one launch (start us, length us, event | category | flops | bytes accessed | tf_op | source)
XLA Modules:
  0.0 57.2 jit_solution(7660071601051345285)
XLA Ops:
  0.7 0.0 copy-start
  0.7 0.7 %copy-done = s32[6,2]{0,1:T(2,128)S(1)} copy-done((s32[6,2]{0,1:T(2,128)S(1)}, s32[6,2]{0,1:T(2,128)}, u32[]{:S(2)}) %copy-start) | copy-done | bytes 72
  1.3 0.7 %copy.8.window_ref = s32[6,2]{1,0:T(8,128)} copy(s32[6,2]{0,1:T(2,128)S(1)} %copy-done) | data formatting | bytes 96 | tf_op args[3]
  2.0 53.5 %exchange_attend.1 = bf16[256,768]{1,0:T(8,128)(2,1)} custom-call(s32[6,2]{1,0:T(8,128)} %copy.8.window_ref, s32[1]{0:T(128)S(6)} %copy.10.text_len_ref, bf16[256,768]{1,0:T(8,128)(2,1)} %bitcast.5, bf16[256,768]{1,0:T(8,128)(2,1)} %bitcast.6, bf16[256,768]{1,0:T(8,128)(2,1)} %bitcast.7, bf16[64,768]{1,0:T(8,128)(2,1)} %tk_ref.1, bf16[64,768]{1,0:T(8,128)(2,1)} %tv_ref.1), custom_call_target="tpu_custom_call" | custom-call | flops 1006632960 | bytes 6291456 | tf_op jit(solution)/shard_map/exchange_attend/pallas_call | solution.py:367
  55.5 1.8 %copy.11 = bf16[1,1,256,768]{3,2,1,0:T(8,128)(2,1)} copy(bf16[1,1,256,768]{3,2,1,0:T(8,128)(2,1)} %bitcast.4) | data formatting | bytes 786432
Async XLA Ops:
  0.7 0.7 %copy-start = (s32[6,2]{0,1:T(2,128)S(1)}, s32[6,2]{0,1:T(2,128)}, u32[]{:S(2)}) copy-start(s32[6,2]{0,1:T(2,128)} %param.10) | copy-start | bytes 148

commit v2 on v0

--- a/solution.py
+++ b/solution.py
@@ -1,9 +1,16 @@
+import functools
 import math
 
 import jax
 import jax.numpy as jnp
 from jax import lax
+from jax.experimental import pallas as pl
+from jax.experimental.pallas import tpu as pltpu
 from jax.sharding import PartitionSpec as P
+
+MESH = pl.DeviceIdType.MESH
+MASKED = -1e30
+VMEM_BUDGET = 24 * 2**20
 
 
 def absorb(softmax_state, query_heads, block_keys, block_values, allowed):
@@ -28,7 +35,7 @@
     return (new_max, running_sum, weighted)
 
 
-def shards(
+def gathered(
     video_queries, video_keys, video_values, head_window, prompt_keys, prompt_values, text_len
 ):
     slab_count = video_queries.shape[0]
@@ -87,6 +94,283 @@
     return result.reshape(slab_count, 1, tile_tok, features).astype(jnp.bfloat16)
 
 
+def attend(queries, blocks, score_scale):
+    scores = [
+        lax.dot_general(
+            queries, keys, (((1,), (1,)), ((), ())), preferred_element_type=jnp.float32
+        )
+        + bias
+        for keys, _, bias in blocks
+    ]
+    row_max = jnp.max(functools.reduce(jnp.maximum, scores), axis=-1, keepdims=True)
+    weights = [jnp.exp2((block - row_max) * (score_scale / math.log(2.0))) for block in scores]
+    row_sum = jnp.sum(functools.reduce(jnp.add, weights), axis=-1, keepdims=True)
+    weighted = functools.reduce(
+        jnp.add,
+        [
+            jnp.dot(weight.astype(jnp.bfloat16), values, preferred_element_type=jnp.float32)
+            for weight, (_, values, _) in zip(weights, blocks)
+        ],
+    )
+    return (weighted * (1.0 / row_sum)).astype(jnp.bfloat16)
+
+def exchange_kernel(
+    dims,
+    window_ref, text_len_ref, q_ref, k_ref, v_ref, tk_ref, tv_ref, out_ref,
+    k_own, tk_own, q_own, v_own, tv_own, o_own, o_land,
+    k_ext, tk_ext, q_ext, v_ext, tv_ext, o_ext, x_land,
+    own_send, own_recv, o_send, o_recv,
+    ext_send, ext_recv, x_send, x_recv, local_sem,
+):
+    n, heads, head_dim, grid_cols = dims
+    me = lax.axis_index("region")
+    odd = lax.axis_index("head") % 2
+    per_device = heads // n
+    extra = heads - per_device * n
+    width = per_device * head_dim
+    half = n // 2
+    side, place = me // half, me % half
+    score_scale = 1.0 / math.sqrt(head_dim)
+    peers = [(1 - side) * half + lax.rem(place + j, half) for j in range(half)]
+    peers += [side * half + lax.rem(place + j, half) for j in range(1, half)]
+
+    barrier = pltpu.get_barrier_semaphore()
+    for peer in peers:
+        pl.semaphore_signal(barrier, inc=1, device_id={"region": peer}, device_id_type=MESH)
+
+    def extra_owner(e):
+        return jnp.where(odd == 0, e, n - 1 - e)
+
+    my_extra = jnp.where(odd == 0, me, n - 1 - me)
+    inputs = (k_ref, tk_ref, q_ref, v_ref, tv_ref)
+    own_bufs = (k_own, tk_own, q_own, v_own, tv_own)
+    ext_bufs = (k_ext, tk_ext, q_ext, v_ext, tv_ext)
+    parts = range(5)
+
+    def own_cols(owner):
+        return pl.ds(pl.multiple_of(owner * width, head_dim), width)
+
+    def ext_cols(e):
+        return pl.ds(pl.multiple_of(n * width + e * head_dim, head_dim), head_dim)
+
+    def remote(src, dst, send_sem, recv_sem, target):
+        return pltpu.make_async_remote_copy(
+            src_ref=src,
+            dst_ref=dst,
+            send_sem=send_sem,
+            recv_sem=recv_sem,
+            device_id={"region": target},
+            device_id_type=MESH,
+        )
+
+    def own_copy(target, source, j, i):
+        return remote(
+            inputs[i].at[:, own_cols(target)],
+            own_bufs[i].at[source],
+            own_send.at[j, i],
+            own_recv.at[source, i],
+            target,
+        )
+
+    def ext_copy(e, target, source, i):
+        return remote(
+            inputs[i].at[:, ext_cols(e)],
+            ext_bufs[i].at[source],
+            ext_send.at[e, i],
+            ext_recv.at[source, i],
+            target,
+        )
+
+    def o_copy(target, source, j):
+        return remote(o_own.at[target], o_land.at[source], o_send.at[j], o_recv.at[source], target)
+
+    def x_copy(e, target, j):
+        return remote(o_ext.at[target], x_land.at[e], x_send.at[j], x_recv.at[e], target)
+
+    local = [
+        pltpu.make_async_copy(inputs[i].at[:, own_cols(me)], own_bufs[i].at[me], local_sem.at[i])
+        for i in parts
+    ]
+    for copy in local:
+        copy.start()
+    local_ext = []
+    if extra:
+        local_ext = [
+            pltpu.make_async_copy(
+                inputs[i].at[:, ext_cols(lax.rem(my_extra, extra))],
+                ext_bufs[i].at[me],
+                local_sem.at[5 + i],
+            )
+            for i in parts
+        ]
+        for copy in local_ext:
+            copy.start()
+
+    pl.semaphore_wait(barrier, n - 1)
+    for e in range(extra):
+
+        @pl.when(me != extra_owner(e))
+        def _(e=e):
+            for i in parts:
+                ext_copy(e, extra_owner(e), me, i).start()
+
+    for j, peer in enumerate(peers):
+        for i in parts:
+            own_copy(peer, me, j, i).start()
+
+    text_bias = jnp.where(
+        lax.broadcasted_iota(jnp.int32, (1, n * tk_ref.shape[0]), 1) < text_len_ref[0], 0.0, MASKED
+    )
+
+    def tile_bias(head, tile_q, tile_k):
+        rows = jnp.abs(tile_q // grid_cols - tile_k // grid_cols)
+        cols = jnp.abs(tile_q % grid_cols - tile_k % grid_cols)
+        within = (rows <= window_ref[0, head]) & (cols <= window_ref[1, head])
+        return jnp.where(within, 0.0, MASKED)
+
+    def tile_attend(bufs, slot, head, tile):
+        keys, text_keys, queries, values, text_values = bufs
+        lanes = pl.ds(slot * head_dim, head_dim)
+        blocks = [(keys[t, :, lanes], values[t, :, lanes], tile_bias(head, tile, t)) for t in range(n)]
+        blocks.append(
+            (
+                text_keys[:, :, lanes].reshape(-1, head_dim),
+                text_values[:, :, lanes].reshape(-1, head_dim),
+                text_bias,
+            )
+        )
+        return attend(queries[tile, :, lanes], blocks, score_scale)
+
+    for copy in local + local_ext:
+        copy.wait()
+    if extra:
+
+        @pl.when(my_extra < extra)
+        def _():
+            for peer in peers:
+                for i in parts:
+                    ext_copy(my_extra, me, peer, i).wait_recv()
+            for j, peer in enumerate(peers):
+                o_ext[peer] = tile_attend(ext_bufs, 0, n * per_device + my_extra, peer)
+                x_copy(my_extra, peer, j).start()
+            x_land[my_extra] = tile_attend(ext_bufs, 0, n * per_device + my_extra, me)
+
+    for peer in peers:
+        for i in parts:
+            own_copy(me, peer, 0, i).wait_recv()
+    for j, peer in enumerate(peers):
+        for slot in range(per_device):
+            o_own[peer, :, pl.ds(slot * head_dim, head_dim)] = tile_attend(
+                own_bufs, slot, me * per_device + slot, peer
+            )
+        o_copy(peer, me, j).start()
+    for slot in range(per_device):
+        o_land[me, :, pl.ds(slot * head_dim, head_dim)] = tile_attend(
+            own_bufs, slot, me * per_device + slot, me
+        )
+
+    for e in range(extra):
+
+        @pl.when(me != extra_owner(e))
+        def _(e=e):
+            x_copy(e, me, 0).wait_recv()
+
+        out_ref[:, pl.ds(n * width + e * head_dim, head_dim)] = x_land[e]
+    for peer in peers:
+        o_copy(me, peer, 0).wait_recv()
+    for owner in range(n):
+        out_ref[:, pl.ds(owner * width, width)] = o_land[owner]
+
+    for j, peer in enumerate(peers):
+        for i in parts:
+            own_copy(peer, me, j, i).wait_send()
+        o_copy(peer, me, j).wait_send()
+    for e in range(extra):
+
+        @pl.when(me != extra_owner(e))
+        def _(e=e):
+            for i in parts:
+                ext_copy(e, extra_owner(e), me, i).wait_send()
+
+    if extra:
+
+        @pl.when(my_extra < extra)
+        def _():
+            for j, peer in enumerate(peers):
+                x_copy(my_extra, peer, j).wait_send()
+
+
+def exchange(
+    video_queries, video_keys, video_values, head_window, prompt_keys, prompt_values, text_len
+):
+    n = lax.axis_size("region")
+    tile_tok, features = video_queries.shape[2:]
+    text_tok = prompt_keys.shape[0]
+    heads = head_window.shape[0]
+    head_dim = features // heads
+    width = heads // n * head_dim
+    extra = max(heads % n, 1)
+    grid_cols = min(8, n // 2)
+    kind = video_queries.dtype
+    any_spec = pl.BlockSpec(memory_space=pl.ANY)
+    smem_spec = pl.BlockSpec(memory_space=pltpu.SMEM)
+    tile_own = pltpu.VMEM((n, tile_tok, width), kind)
+    text_own = pltpu.VMEM((n, text_tok, width), kind)
+    tile_ext = pltpu.VMEM((n, tile_tok, head_dim), kind)
+    text_ext = pltpu.VMEM((n, text_tok, head_dim), kind)
+    dma = pltpu.SemaphoreType.DMA
+    keys_total = n * (tile_tok + text_tok)
+    result = pl.pallas_call(
+        functools.partial(exchange_kernel, (n, heads, head_dim, grid_cols)),
+        out_shape=jax.ShapeDtypeStruct((tile_tok, features), kind),
+        in_specs=[smem_spec, smem_spec] + [any_spec] * 5,
+        out_specs=pl.BlockSpec(memory_space=pltpu.VMEM),
+        scratch_shapes=[
+            tile_own, text_own, tile_own, tile_own, text_own, tile_own, tile_own,
+            tile_ext, text_ext, tile_ext, tile_ext, text_ext, tile_ext,
+            pltpu.VMEM((extra, tile_tok, head_dim), kind),
+            dma((n, 5)), dma((n, 5)), dma((n,)), dma((n,)),
+            dma((extra, 5)), dma((n, 5)), dma((n,)), dma((extra,)), dma((10,)),
+        ],
+        compiler_params=pltpu.CompilerParams(collective_id=0, has_side_effects=True),
+        cost_estimate=pl.CostEstimate(
+            flops=4 * tile_tok * features * keys_total,
+            bytes_accessed=8 * tile_tok * features * n,
+            transcendentals=tile_tok * heads * keys_total,
+        ),
+        name="exchange_attend",
+    )(
+        head_window.T,
+        text_len,
+        video_queries.reshape(tile_tok, features),
+        video_keys.reshape(tile_tok, features),
+        video_values.reshape(tile_tok, features),
+        prompt_keys,
+        prompt_values,
+    )
+    return result.reshape(video_queries.shape)
+
+
+def fits(video_queries, head_window):
+    n = lax.axis_size("region")
+    heads = head_window.shape[0]
+    slabs, tiles, tile_tok, features = video_queries.shape
+    landed = 12 * n * tile_tok * features
+    return (
+        slabs == 1 and tiles == 1 and n % 2 == 0 and heads >= n
+        and features // heads == 128 and landed < VMEM_BUDGET
+    )
+
+
+def shards(
+    video_queries, video_keys, video_values, head_window, prompt_keys, prompt_values, text_len
+):
+    route = exchange if fits(video_queries, head_window) else gathered
+    return route(
+        video_queries, video_keys, video_values, head_window, prompt_keys, prompt_values, text_len
+    )
+
+
 def solution(mesh):
     in_specs = (
         P("groups", "region", None, "head"),

time: 108 us -> 50.4 us (0.47)
  Pallas kernels: 0 us -> 47.8 us
  blocking collectives: 38.2 us -> 0 us
  waiting for transfers between devices: 33.3 us -> 0 us
  between operations: 14.2 us -> 0.66 us
  local copies, waits for them, and re-layouts: 9.24 us -> 1.77 us
  other arithmetic: 4.98 us -> 0 us
  matrix products: 4.77 us -> 0 us
  loops' own time: 3.17 us -> 0 us
    pallas_call x0 -> x1, Pallas kernels: none -> 47.8 us  [exchange(): pl.pallas_call(functools.partial(exchange_kernel, (n, heads, head_dim, gr...]
    all_gather x2 -> x0, blocking collectives: 38.2 us -> none  [the longest x1 20.2 us: shards(): lax.all_gather(prompt_values, 'region', axis=0, tiled=True)]
    all_gather x1 -> x0, waiting for transfers between devices: 33.3 us -> none  [shards(): shard_piece = lax.all_gather(paired, 'region', axis=2, tiled=True)]
    dot_general x10 -> x0, matrix products: 4.77 us -> none  [the longest x5 2.63 us: absorb(): jnp.einsum('shqk,skhd->sqhd', weights.astype(jnp.bfloat16), block_values,...]
    slice x4 -> x0, local copies, waits for them, and re-layouts: 4.7 us -> none  [one_tile(): tile_pair[1].reshape(slab_count, tile_tok, head_count, head_dim)]
    another operation x5 -> x0, loops' own time: 3.17 us -> none  [the longest x1 2.89 us: shards(): softmax_state = lax.fori_loop(0, piece_count, one_tile, softmax_state)]
    reduce_or x4 -> x0, other arithmetic: 2.79 us -> none  [one_tile(): return lax.cond(jnp.any(within), take_tile, keep_state, state_in)]
    unnamed x11 -> x1, local copies, waits for them, and re-layouts: 2.98 us -> 1.77 us
  transfers between devices with their start and end apart: 1 -> 0, of which waited for: 1 -> 0; matrix products, arithmetic and copies ran while one was open for 1% -> 0% of each run, Pallas kernels for 0% -> 0%
where the time goes in v2:
time: 50.4 us; the launch traced here: 50.2 us
  Pallas kernels  47.8 us (95%)
  local copies, waits for them, and re-layouts  1.77 us (4%)
  between operations  0.66 us (1%)
    pallas_call x1, Pallas kernels, exchange(): pl.pallas_call(functools.partial(exchange_kernel, (n, heads, head_dim, gr...  47.8 us
    unnamed x1, local copies, waits for them, and re-layouts  1.77 us

profile of v2, /device:TPU:0, one launch (start us, length us, event | category | flops | bytes accessed | tf_op | source)
XLA Modules:
  0.0 50.2 jit_solution(632505542851383361)
XLA Ops:
  0.7 47.8 %exchange_attend.1 = bf16[256,768]{1,0:T(8,128)(2,1)} custom-call(s32[2,6]{1,0:T(2,128)} %bitcast.9, s32[1]{0:T(128)S(6)} %copy.9.text_len_ref, bf16[256,768]{1,0:T(8,128)(2,1)} %bitcast.6, bf16[256,768]{1,0:T(8,128)(2,1)} %bitcast.7, bf16[256,768]{1,0:T(8,128)(2,1)} %bitcast.8, bf16[64,768]{1,0:T(8,128)(2,1)} %tk_ref.1, bf16[64,768]{1,0:T(8,128)(2,1)} %tv_ref.1), custom_call_target="tpu_custom_call" | custom-call | flops 1006632960 | bytes 6291456 | tf_op jit(solution)/shard_map/exchange_attend/pallas_call | solution.py:323
  48.4 1.8 %copy.10 = bf16[1,1,256,768]{3,2,1,0:T(8,128)(2,1)} copy(bf16[1,1,256,768]{3,2,1,0:T(8,128)(2,1)} %bitcast.5) | data formatting | bytes 786432

commit v3 on v2

--- a/solution.py
+++ b/solution.py
@@ -116,9 +116,9 @@
 
 def exchange_kernel(
     dims,
-    window_ref, text_len_ref, q_ref, k_ref, v_ref, tk_ref, tv_ref, out_ref,
-    k_own, tk_own, q_own, v_own, tv_own, o_own, o_land,
-    k_ext, tk_ext, q_ext, v_ext, tv_ext, o_ext, x_land,
+    window_ref, text_len_ref, q_ref, k_ref, v_ref, tk_ref, tv_ref, o_fin, x_fin,
+    k_own, tk_own, v_own, tv_own, q_own, o_own, o_land,
+    k_ext, tk_ext, v_ext, tv_ext, q_ext, o_ext, x_land,
     own_send, own_recv, o_send, o_recv,
     ext_send, ext_recv, x_send, x_recv, local_sem,
 ):
@@ -134,6 +134,11 @@
     peers = [(1 - side) * half + lax.rem(place + j, half) for j in range(half)]
     peers += [side * half + lax.rem(place + j, half) for j in range(1, half)]
 
+    def peer_at(j):
+        across = j < half
+        there = jnp.where(across, 1 - side, side)
+        return there * half + lax.rem(place + jnp.where(across, j, j - half + 1), half)
+
     barrier = pltpu.get_barrier_semaphore()
     for peer in peers:
         pl.semaphore_signal(barrier, inc=1, device_id={"region": peer}, device_id_type=MESH)
@@ -142,10 +147,10 @@
         return jnp.where(odd == 0, e, n - 1 - e)
 
     my_extra = jnp.where(odd == 0, me, n - 1 - me)
-    inputs = (k_ref, tk_ref, q_ref, v_ref, tv_ref)
-    own_bufs = (k_own, tk_own, q_own, v_own, tv_own)
-    ext_bufs = (k_ext, tk_ext, q_ext, v_ext, tv_ext)
-    parts = range(5)
+    inputs = (k_ref, tk_ref, v_ref, tv_ref, q_ref)
+    own_bufs = (k_own, tk_own, v_own, tv_own, q_own)
+    ext_bufs = (k_ext, tk_ext, v_ext, tv_ext, q_ext)
+    parts, key_parts, query_part = range(5), range(4), 4
 
     def own_cols(owner):
         return pl.ds(pl.multiple_of(owner * width, head_dim), width)
@@ -207,16 +212,20 @@
             copy.start()
 
     pl.semaphore_wait(barrier, n - 1)
-    for e in range(extra):
-
-        @pl.when(me != extra_owner(e))
-        def _(e=e):
-            for i in parts:
-                ext_copy(e, extra_owner(e), me, i).start()
-
     for j, peer in enumerate(peers):
-        for i in parts:
+        for i in key_parts:
             own_copy(peer, me, j, i).start()
+    for j, peer in enumerate(peers):
+        own_copy(peer, me, j, query_part).start()
+
+    for pieces in (key_parts, (query_part,)):
+        for e in range(extra):
+
+            @pl.when(me != extra_owner(e))
+            def _(e=e, pieces=pieces):
+                for i in pieces:
+                    ext_copy(e, extra_owner(e), me, i).start()
+
 
     text_bias = jnp.where(
         lax.broadcasted_iota(jnp.int32, (1, n * tk_ref.shape[0]), 1) < text_len_ref[0], 0.0, MASKED
@@ -229,7 +238,7 @@
         return jnp.where(within, 0.0, MASKED)
 
     def tile_attend(bufs, slot, head, tile):
-        keys, text_keys, queries, values, text_values = bufs
+        keys, text_keys, values, text_values, queries = bufs
         lanes = pl.ds(slot * head_dim, head_dim)
         blocks = [(keys[t, :, lanes], values[t, :, lanes], tile_bias(head, tile, t)) for t in range(n)]
         blocks.append(
@@ -243,31 +252,59 @@
 
     for copy in local + local_ext:
         copy.wait()
+    def own_tile(out, tile):
+        for slot in range(per_device):
+            out[:, pl.ds(slot * head_dim, head_dim)] = tile_attend(
+                own_bufs, slot, me * per_device + slot, tile
+            )
+
+    for peer in peers:
+        for i in key_parts:
+            own_copy(me, peer, 0, i).wait_recv()
+
+    def own_step(j, _):
+        peer = peer_at(j)
+
+        @pl.when(j < n - 1)
+        def _():
+            own_copy(me, peer, 0, query_part).wait_recv()
+
+        own_tile(o_own.at[peer], peer)
+
+        @pl.when(j < n - 1)
+        def _():
+            o_copy(peer, me, j).start()
+
+        return 0
+
+    lax.fori_loop(0, n, own_step, 0)
+
     if extra:
 
         @pl.when(my_extra < extra)
         def _():
+            head = n * per_device + my_extra
             for peer in peers:
-                for i in parts:
+                for i in key_parts:
                     ext_copy(my_extra, me, peer, i).wait_recv()
-            for j, peer in enumerate(peers):
-                o_ext[peer] = tile_attend(ext_bufs, 0, n * per_device + my_extra, peer)
-                x_copy(my_extra, peer, j).start()
-            x_land[my_extra] = tile_attend(ext_bufs, 0, n * per_device + my_extra, me)
-
-    for peer in peers:
-        for i in parts:
-            own_copy(me, peer, 0, i).wait_recv()
-    for j, peer in enumerate(peers):
-        for slot in range(per_device):
-            o_own[peer, :, pl.ds(slot * head_dim, head_dim)] = tile_attend(
-                own_bufs, slot, me * per_device + slot, peer
-            )
-        o_copy(peer, me, j).start()
-    for slot in range(per_device):
-        o_land[me, :, pl.ds(slot * head_dim, head_dim)] = tile_attend(
-            own_bufs, slot, me * per_device + slot, me
-        )
+
+            def ext_step(j, _):
+                peer = peer_at(j)
+
+                @pl.when(j < n - 1)
+                def _():
+                    ext_copy(my_extra, me, peer, query_part).wait_recv()
+
+                o_ext[peer] = tile_attend(ext_bufs, 0, head, peer)
+
+                @pl.when(j < n - 1)
+                def _():
+                    x_copy(my_extra, peer, j).start()
+
+                return 0
+
+            lax.fori_loop(0, n, ext_step, 0)
+            x_land[my_extra] = o_ext[me]
 
     for e in range(extra):
 
@@ -275,11 +312,12 @@
         def _(e=e):
             x_copy(e, me, 0).wait_recv()
 
-        out_ref[:, pl.ds(n * width + e * head_dim, head_dim)] = x_land[e]
+        x_fin[:, pl.ds(e * head_dim, head_dim)] = x_land[e]
     for peer in peers:
         o_copy(me, peer, 0).wait_recv()
+    o_land[me] = o_own[me]
     for owner in range(n):
-        out_ref[:, pl.ds(owner * width, width)] = o_land[owner]
+        o_fin[:, pl.ds(owner * width, width)] = o_land[owner]
 
     for j, peer in enumerate(peers):
         for i in parts:
@@ -298,6 +336,11 @@
         def _():
             for j, peer in enumerate(peers):
                 x_copy(my_extra, peer, j).wait_send()
+
+
+def assemble_kernel(split, own_ref, ext_ref, out_ref):
+    out_ref[:, :split] = own_ref[...]
+    out_ref[:, split:] = ext_ref[:, : out_ref.shape[1] - split]
 
 
 def exchange(
@@ -320,14 +363,17 @@
     text_ext = pltpu.VMEM((n, text_tok, head_dim), kind)
     dma = pltpu.SemaphoreType.DMA
     keys_total = n * (tile_tok + text_tok)
-    result = pl.pallas_call(
+    landed = pl.pallas_call(
         functools.partial(exchange_kernel, (n, heads, head_dim, grid_cols)),
-        out_shape=jax.ShapeDtypeStruct((tile_tok, features), kind),
+        out_shape=(
+            pltpu.VMEM((tile_tok, n * width), kind),
+            pltpu.VMEM((tile_tok, extra * head_dim), kind),
+        ),
         in_specs=[smem_spec, smem_spec] + [any_spec] * 5,
-        out_specs=pl.BlockSpec(memory_space=pltpu.VMEM),
+        out_specs=[pl.BlockSpec(memory_space=pltpu.VMEM)] * 2,
         scratch_shapes=[
-            tile_own, text_own, tile_own, tile_own, text_own, tile_own, tile_own,
-            tile_ext, text_ext, tile_ext, tile_ext, text_ext, tile_ext,
+            tile_own, text_own, tile_own, text_own, tile_own, tile_own, tile_own,
+            tile_ext, text_ext, tile_ext, text_ext, tile_ext, tile_ext,
             pltpu.VMEM((extra, tile_tok, head_dim), kind),
             dma((n, 5)), dma((n, 5)), dma((n,)), dma((n,)),
             dma((extra, 5)), dma((n, 5)), dma((n,)), dma((extra,)), dma((10,)),
@@ -348,6 +394,13 @@
         prompt_keys,
         prompt_values,
     )
+    result = pl.pallas_call(
+        functools.partial(assemble_kernel, n * width),
+        out_shape=jax.ShapeDtypeStruct((tile_tok, features), kind),
+        in_specs=[pl.BlockSpec(memory_space=pltpu.VMEM)] * 2,
+        out_specs=pl.BlockSpec(memory_space=pltpu.VMEM),
+        name="assemble",
+    )(*[pltpu.with_memory_space_constraint(piece, pltpu.VMEM) for piece in landed])
     return result.reshape(video_queries.shape)
 
 

time: 50.4 us -> 48.4 us (0.960)
  local copies, waits for them, and re-layouts: 1.77 us -> 0 us
    unnamed x1 -> x0, local copies, waits for them, and re-layouts: 1.77 us -> none
    pallas_call x1, Pallas kernels: 47.8 us -> 46.8 us  [exchange(): pl.pallas_call(functools.partial(exchange_kernel, (n, heads, head_dim, gr...]
    pallas_call x0 -> x1, Pallas kernels: none -> 0.77 us  [exchange(): pl.pallas_call(functools.partial(assemble_kernel, n * width), out_shape=j...]
where the time goes in v3:
time: 48.4 us; the launch traced here: 48.2 us
  Pallas kernels  47.5 us (98%)
  between operations  0.66 us (1%)
    pallas_call x1, Pallas kernels, exchange(): pl.pallas_call(functools.partial(exchange_kernel, (n, heads, head_dim, gr...  46.8 us

profile of v3, /device:TPU:0, one launch (start us, length us, event | category | flops | bytes accessed | tf_op | source)
XLA Modules:
  0.0 48.2 jit_solution(494116509817549221)
XLA Ops:
  0.7 46.8 %exchange_attend.1 = (bf16[256,512]{1,0:T(8,128)(2,1)S(1)}, bf16[256,256]{1,0:T(8,128)(2,1)S(1)}) custom-call(s32[2,6]{1,0:T(2,128)} %bitcast.8, s32[1]{0:T(128)S(6)} %copy.8.text_len_ref, bf16[256,768]{1,0:T(8,128)(2,1)} %bitcast.5, bf16[256,768]{1,0:T(8,128)(2,1)} %bitcast.6, bf16[256,768]{1,0:T(8,128)(2,1)} %bitcast.7, bf16[64,768]{1,0:T(8,128)(2,1)} %tk_ref.1, ...), custom_call_target="tpu_custom_call" | custom-call | flops 1006632960 | bytes 6291456 | tf_op jit(solution)/shard_map/exchange_attend/pallas_call | solution.py:366
  47.4 0.8 %assemble.1 = bf16[256,768]{1,0:T(8,128)(2,1)} custom-call(bf16[256,512]{1,0:T(8,128)(2,1)S(1)} %get-tuple-element.7.own_ref, bf16[256,256]{1,0:T(8,128)(2,1)S(1)} %get-tuple-element.8.ext_ref), custom_call_target="tpu_custom_call" | custom-call | tf_op jit(solution)/shard_map/assemble/pallas_call | solution.py:397

commit v4 on v3

--- a/solution.py
+++ b/solution.py
@@ -117,8 +117,8 @@
 def exchange_kernel(
     dims,
     window_ref, text_len_ref, q_ref, k_ref, v_ref, tk_ref, tv_ref, o_fin, x_fin,
-    k_own, tk_own, v_own, tv_own, q_own, o_own, o_land,
-    k_ext, tk_ext, v_ext, tv_ext, q_ext, o_ext, x_land,
+    k_own, tk_own, v_own, tv_own, q_own, o_own,
+    k_ext, tk_ext, v_ext, tv_ext, q_ext, o_ext,
     own_send, own_recv, o_send, o_recv,
     ext_send, ext_recv, x_send, x_recv, local_sem,
 ):
@@ -158,6 +158,9 @@
     def ext_cols(e):
         return pl.ds(pl.multiple_of(n * width + e * head_dim, head_dim), head_dim)
 
+    def fin_cols(e):
+        return pl.ds(pl.multiple_of(e * head_dim, head_dim), head_dim)
+
     def remote(src, dst, send_sem, recv_sem, target):
         return pltpu.make_async_remote_copy(
             src_ref=src,
@@ -187,10 +190,18 @@
         )
 
     def o_copy(target, source, j):
-        return remote(o_own.at[target], o_land.at[source], o_send.at[j], o_recv.at[source], target)
+        return remote(
+            o_own.at[target],
+            o_fin.at[:, own_cols(source)],
+            o_send.at[j],
+            o_recv.at[source],
+            target,
+        )
 
     def x_copy(e, target, j):
-        return remote(o_ext.at[target], x_land.at[e], x_send.at[j], x_recv.at[e], target)
+        return remote(
+            o_ext.at[target], x_fin.at[:, fin_cols(e)], x_send.at[j], x_recv.at[e], target
+        )
 
     local = [
         pltpu.make_async_copy(inputs[i].at[:, own_cols(me)], own_bufs[i].at[me], local_sem.at[i])
@@ -304,7 +315,7 @@
                 return 0
 
             lax.fori_loop(0, n, ext_step, 0)
-            x_land[my_extra] = o_ext[me]
+            x_fin[:, fin_cols(my_extra)] = o_ext[me]
 
     for e in range(extra):
 
@@ -312,12 +323,9 @@
         def _(e=e):
             x_copy(e, me, 0).wait_recv()
 
-        x_fin[:, pl.ds(e * head_dim, head_dim)] = x_land[e]
     for peer in peers:
         o_copy(me, peer, 0).wait_recv()
-    o_land[me] = o_own[me]
-    for owner in range(n):
-        o_fin[:, pl.ds(owner * width, width)] = o_land[owner]
+    o_fin[:, own_cols(me)] = o_own[me]
 
     for j, peer in enumerate(peers):
         for i in parts:
@@ -338,9 +346,16 @@
                 x_copy(my_extra, peer, j).wait_send()
 
 
-def assemble_kernel(split, own_ref, ext_ref, out_ref):
-    out_ref[:, :split] = own_ref[...]
-    out_ref[:, split:] = ext_ref[:, : out_ref.shape[1] - split]
+def assemble_kernel(own_ref, ext_ref, out_ref, sems):
+    split, features = own_ref.shape[1], out_ref.shape[1]
+    copies = [pltpu.make_async_copy(own_ref, out_ref.at[:, pl.ds(0, split)], sems.at[0])]
+    if features > split:
+        rest = pl.ds(split, features - split)
+        copies.append(pltpu.make_async_copy(ext_ref, out_ref.at[:, rest], sems.at[1]))
+    for copy in copies:
+        copy.start()
+    for copy in copies:
+        copy.wait()
 
 
 def exchange(
@@ -372,9 +387,8 @@
         in_specs=[smem_spec, smem_spec] + [any_spec] * 5,
         out_specs=[pl.BlockSpec(memory_space=pltpu.VMEM)] * 2,
         scratch_shapes=[
-            tile_own, text_own, tile_own, text_own, tile_own, tile_own, tile_own,
+            tile_own, text_own, tile_own, text_own, tile_own, tile_own,
             tile_ext, text_ext, tile_ext, text_ext, tile_ext, tile_ext,
-            pltpu.VMEM((extra, tile_tok, head_dim), kind),
             dma((n, 5)), dma((n, 5)), dma((n,)), dma((n,)),
             dma((extra, 5)), dma((n, 5)), dma((n,)), dma((extra,)), dma((10,)),
         ],
@@ -395,10 +409,11 @@
         prompt_values,
     )
     result = pl.pallas_call(
-        functools.partial(assemble_kernel, n * width),
+        assemble_kernel,
         out_shape=jax.ShapeDtypeStruct((tile_tok, features), kind),
         in_specs=[pl.BlockSpec(memory_space=pltpu.VMEM)] * 2,
-        out_specs=pl.BlockSpec(memory_space=pltpu.VMEM),
+        out_specs=any_spec,
+        scratch_shapes=[dma((2,))],
         name="assemble",
     )(*[pltpu.with_memory_space_constraint(piece, pltpu.VMEM) for piece in landed])
     return result.reshape(video_queries.shape)

time: 48.4 us -> 48.3 us (level)
  no operation moved by 1% of the time
where the time goes in v4:
time: 48.3 us; the launch traced here: 48.2 us
  Pallas kernels  47.5 us (98%)
  between operations  0.66 us (1%)
    pallas_call x1, Pallas kernels, exchange(): pl.pallas_call(functools.partial(exchange_kernel, (n, heads, head_dim, gr...  46.7 us

profile of v4, /device:TPU:0, one launch (start us, length us, event | category | flops | bytes accessed | tf_op | source)
XLA Modules:
  0.0 48.2 jit_solution(16982340339730082771)
XLA Ops:
  0.7 46.7 %exchange_attend.1 = (bf16[256,512]{1,0:T(8,128)(2,1)S(1)}, bf16[256,256]{1,0:T(8,128)(2,1)S(1)}) custom-call(s32[2,6]{1,0:T(2,128)} %bitcast.8, s32[1]{0:T(128)S(6)} %copy.8.text_len_ref, bf16[256,768]{1,0:T(8,128)(2,1)} %bitcast.5, bf16[256,768]{1,0:T(8,128)(2,1)} %bitcast.6, bf16[256,768]{1,0:T(8,128)(2,1)} %bitcast.7, bf16[64,768]{1,0:T(8,128)(2,1)} %tk_ref.1, ...), custom_call_target="tpu_custom_call" | custom-call | flops 1006632960 | bytes 6291456 | tf_op jit(solution)/shard_map/exchange_attend/pallas_call | solution.py:381
  47.4 0.8 %assemble.1 = bf16[256,768]{1,0:T(8,128)(2,1)} custom-call(bf16[256,512]{1,0:T(8,128)(2,1)S(1)} %get-tuple-element.7.own_ref, bf16[256,256]{1,0:T(8,128)(2,1)S(1)} %get-tuple-element.8.ext_ref), custom_call_target="tpu_custom_call" | custom-call | tf_op jit(solution)/shard_map/assemble/pallas_call | solution.py:411
